TPU v7x, 256 devices: a whole 4x4x8 slice. The times are simulated.
256 devices in a mesh: pb: 16 (over x, z_hi), sa: 16 (over z_lo, y, core).
Axes of the slice: x: 4, y: 4, z: 8 (z_hi: 4, z_lo: 2; z = z_hi * 2 + z_lo), core: 2. Of those that a mesh axis runs over, the one named last changes fastest.
Arguments:
- question_states: bfloat16 [16, 16, 256, 768], P('pb', 'sa'), may hold values from -16 to 16
- question_ids: int32 [16, 16, 256], P('pb'), may hold values from 0 to 30521, as said below
- q_inner_weight: bfloat16 [768, 3072], P(None, 'sa'), may hold values from -0.21875 to 0.21875
- q_outer_weight: bfloat16 [3072, 768], P('sa'), may hold values from -0.109375 to 0.109375
- q_norm_gain: float32 [768], replicated, may hold values from 0.1 to 1.9
- sql_states: bfloat16 [16, 16, 256, 768], P('sa', 'pb'), may hold values from -16 to 16
- sql_ids: int32 [16, 16, 256], P('sa'), may hold values from 0 to 32099, as said below
- s_inner_weight: bfloat16 [768, 3072], P(None, 'pb'), may hold values from -0.21875 to 0.21875
- s_outer_weight: bfloat16 [3072, 768], P('pb'), may hold values from -0.109375 to 0.109375
- s_norm_gain: float32 [768], replicated, may hold values from 0.1 to 1.9
- positive_column: int32 [256], P('pb'), may hold values from 0 to 255, each once
Outputs:
- loss: float32 [], replicated
- q_inner_grad: float32 [768, 3072], P(None, 'sa')
- q_outer_grad: float32 [3072, 768], P('sa')
- q_gain_grad: float32 [768], replicated
- s_inner_grad: float32 [768, 3072], P(None, 'pb')
- s_outer_grad: float32 [3072, 768], P('pb')
- s_gain_grad: float32 [768], replicated
Inputs may be any that keep to these rules, and one draw needn't show every extreme that they name: `question_ids`: each sequence is a run of nonzero ids followed by padding zeros, the run 3 * 64 long or longer. `sql_ids`: each sequence is a run of nonzero ids followed by padding zeros, the run 3 * 64 long or longer.
All inputs are finite; a program needn't handle non-finite values.
Results may differ from a plain program's by a relative error of at most 0.0051.
Values may be sent and summed in bfloat16 or wider, within the bound.
A program may use at most 128 MiB of HBM per device.

v0:
```python
import math
import jax
import jax.numpy as jnp
from jax import lax
from jax.sharding import PartitionSpec as P

D = 768
HIGH = lax.Precision.HIGHEST


def apply_rms_norm(input_float, norm_gain_vector, root_mean_square):
    if root_mean_square:
        input_normalized = input_float * lax.rsqrt(
            jnp.mean(input_float * input_float, axis=-1, keepdims=True) + 1e-06
        )
    else:
        mean_removed = input_float - jnp.mean(input_float, axis=-1, keepdims=True)
        input_normalized = mean_removed * lax.rsqrt(
            jnp.mean(mean_removed * mean_removed, axis=-1, keepdims=True) + 1e-05
        )
    return (input_normalized, (input_normalized * norm_gain_vector).astype(jnp.bfloat16))


def gelu_value(v):
    return 0.5 * v * (1.0 + lax.erf(v / math.sqrt(2.0)))


def gelu_slope(v):
    return 0.5 * (1.0 + lax.erf(v / math.sqrt(2.0))) + v * jnp.exp(-0.5 * v * v) / math.sqrt(
        2.0 * math.pi
    )


def pool_weights(ids):
    mask = (ids > 0).astype(jnp.float32)
    return mask / jnp.sum(mask, axis=-1, keepdims=True)


def tower_forward(tokens, ids, inner, gain, root_mean_square):
    count, length, width = tokens.shape
    input_float = tokens.astype(jnp.float32).reshape(count * length, width)
    input_normalized, normalized_rows = apply_rms_norm(input_float, gain, root_mean_square)
    pre = jnp.dot(normalized_rows, inner, preferred_element_type=jnp.float32)
    weights = pool_weights(ids)
    hidden = gelu_value(pre).reshape(count, length, -1)
    pooled = jnp.einsum("nt,ntf->nf", weights, hidden, precision=HIGH)
    resid = jnp.einsum(
        "nt,ntd->nd", weights, input_float.reshape(count, length, width), precision=HIGH
    )
    return (input_normalized, normalized_rows, pre, weights, pooled, resid)


def tower_backward(input_normalized, normalized_rows, pre, weights, inner, hidden_grad):
    count, length = weights.shape
    slope = gelu_slope(pre).reshape(count, length, -1)
    dpre = (
        (weights[:, :, None] * hidden_grad[:, None, :] * slope)
        .reshape(count * length, -1)
        .astype(jnp.bfloat16)
    )
    inner_part = lax.dot_general(
        normalized_rows, dpre, (((0,), (0,)), ((), ())), preferred_element_type=jnp.float32
    )
    normalized_grad = lax.dot_general(
        dpre, inner, (((1,), (1,)), ((), ())), preferred_element_type=jnp.float32
    )
    return (inner_part, jnp.sum(input_normalized * normalized_grad, axis=0))


def per_device(
    question_states,
    question_ids,
    q_inner_weight,
    q_outer_weight,
    q_norm_gain,
    sql_states,
    sql_ids,
    s_inner_weight,
    s_outer_weight,
    s_norm_gain,
    positive_column,
):
    scale = 1.0 / math.sqrt(D)
    q_place = lax.axis_index("sa")
    s_place = lax.axis_index("pb")
    q_tokens = lax.all_gather(question_states, "sa", axis=1, tiled=True)[0]
    s_tokens = lax.all_gather(sql_states, "pb", axis=1, tiled=True)[0]
    q_rows = q_tokens.shape[0]
    s_rows = s_tokens.shape[0]
    q_hat, q_normed, q_pre, q_weights, q_pooled, q_resid = tower_forward(
        q_tokens, question_ids[0], q_inner_weight, q_norm_gain, False
    )
    s_hat, s_normed, s_pre, s_weights, s_pooled, s_resid = tower_forward(
        s_tokens, sql_ids[0], s_inner_weight, s_norm_gain, True
    )
    q_outer_f = q_outer_weight.astype(jnp.float32)
    s_outer_f = s_outer_weight.astype(jnp.float32)
    q_block = lax.psum(jnp.dot(q_pooled, q_outer_f, precision=HIGH), "sa") + q_resid
    s_block = lax.psum(jnp.dot(s_pooled, s_outer_f, precision=HIGH), "pb") + s_resid
    q_embed = lax.all_gather(q_block, "pb", axis=0, tiled=True)
    s_embed = lax.all_gather(s_block, "sa", axis=0, tiled=True)
    q_pooled_all = lax.all_gather(q_pooled, "pb", axis=0, tiled=True)
    s_pooled_all = lax.all_gather(s_pooled, "sa", axis=0, tiled=True)
    positive_all = lax.all_gather(positive_column, "pb", axis=0, tiled=True)
    score = scale * lax.dot_general(q_embed, s_embed, (((1,), (1,)), ((), ())), precision=HIGH)
    count = score.shape[0]
    match = (positive_all[:, None] == jnp.arange(count, dtype=jnp.int32)[None, :]).astype(
        jnp.float32
    )
    row_max = jnp.max(score, axis=1)
    row_lse = row_max + jnp.log(jnp.sum(jnp.exp(score - row_max[:, None]), axis=1))
    col_max = jnp.max(score, axis=0)
    col_lse = col_max + jnp.log(jnp.sum(jnp.exp(score - col_max[None, :]), axis=0))
    row_pos = jnp.sum(match * score, axis=1)
    col_pos = jnp.sum(match * score, axis=0)
    loss = (jnp.sum(row_lse - row_pos) + jnp.sum(col_lse - col_pos)) / (2.0 * count)
    dscore = 0.5 * (
        jnp.exp(score - row_lse[:, None]) + jnp.exp(score - col_lse[None, :]) - 2.0 * match
    )
    q_grad = scale * jnp.dot(dscore, s_embed, precision=HIGH)
    s_grad = scale * lax.dot_general(dscore, q_embed, (((0,), (0,)), ((), ())), precision=HIGH)
    q_outer_grad = lax.dot_general(q_pooled_all, q_grad, (((0,), (0,)), ((), ())), precision=HIGH)
    s_outer_grad = lax.dot_general(s_pooled_all, s_grad, (((0,), (0,)), ((), ())), precision=HIGH)
    q_grad_own = lax.dynamic_slice_in_dim(q_grad, s_place * q_rows, q_rows, 0)
    s_grad_own = lax.dynamic_slice_in_dim(s_grad, q_place * s_rows, s_rows, 0)
    q_hidden_grad = lax.dot_general(q_grad_own, q_outer_f, (((1,), (1,)), ((), ())), precision=HIGH)
    s_hidden_grad = lax.dot_general(s_grad_own, s_outer_f, (((1,), (1,)), ((), ())), precision=HIGH)
    q_inner_part, q_gain_part = tower_backward(
        q_hat, q_normed, q_pre, q_weights, q_inner_weight, q_hidden_grad
    )
    s_inner_part, s_gain_part = tower_backward(
        s_hat, s_normed, s_pre, s_weights, s_inner_weight, s_hidden_grad
    )
    q_inner_grad = lax.psum(q_inner_part, "pb")
    s_inner_grad = lax.psum(s_inner_part, "sa")
    q_gain_grad, s_gain_grad = lax.psum((q_gain_part, s_gain_part), ("pb", "sa"))
    return (loss, q_inner_grad, q_outer_grad, q_gain_grad, s_inner_grad, s_outer_grad, s_gain_grad)


def solution(mesh):
    placed = (
        P("pb", "sa", None, None),
        P("pb", None, None),
        P(None, "sa"),
        P("sa", None),
        P(),
        P("sa", "pb", None, None),
        P("sa", None, None),
        P(None, "pb"),
        P("pb", None),
        P(),
        P("pb"),
    )
    return jax.shard_map(
        per_device,
        mesh=mesh,
        in_specs=placed,
        out_specs=(P(), P(None, "sa"), P("sa", None), P(), P(None, "pb"), P("pb", None), P()),
        check_vma=False,
    )
```

profile of v0, /device:TPU:25, one launch (start us, length us, event | category | flops | bytes accessed | tf_op | source)
XLA Modules:
  0.0 705.5 jit_solution(16623077752459873952)
XLA Ops:
  7.2 0.7 all-gather.5.cloned.1.call-update
  8.0 0.7 all-gather.3.cloned.1.call-update
  8.7 0.7 convert_bitcast_fusion.2
  9.5 0.7 convert_bitcast_fusion
  10.6 1.3 dynamic-slice
  13.8 0.8 dynamic-update-slice
  14.6 18.9 %all-reduce = s32[256]{0:T(256)} all-reduce(s32[256]{0:T(256)S(1)} %dynamic-update-slice), channel_id=1, replica_groups=mesh['pb'=16,'sa'=16] {'pb'}, use_global_device_ids=true, to_apply=%add | all-reduce | flops 256 | bytes 2048
  33.5 70.1 %all-gather.5.cloned.1.call-done = bf16[1,16,256,768]{3,2,0,1:T(8,128)(2,1)} async-done(((bf16[1,1,256,768]{3,2,0,1:T(8,128)(2,1)}), bf16[1,16,256,768]{3,2,0,1:T(8,128)(2,1)}) %all-gather.5.cloned.1.call-update) | async-done | bytes 6291472 | tf_op jit(solution)/shard_map/all_gather | solution.py:87
  103.6 4.1 multiply_reduce_fusion.2
  107.7 48.2 %all-gather.3.cloned.1.call-done = bf16[1,16,256,768]{3,2,0,1:T(8,128)(2,1)} async-done(((bf16[1,1,256,768]{3,2,0,1:T(8,128)(2,1)}), bf16[1,16,256,768]{3,2,0,1:T(8,128)(2,1)}) %all-gather.3.cloned.1.call-update) | async-done | bytes 6291472 | tf_op jit(solution)/shard_map/all_gather | solution.py:86
  155.9 3.8 convert_reduce_fusion
  159.8 0.7 copy-done.1
  160.5 1.9 multiply_reduce_fusion.3
  162.5 0.8 copy-done.2
  163.3 1.5 multiply_convert_fusion
  164.8 3.8 multiply_multiply_fusion.2
  168.6 2.7 fusion.17
  171.3 0.6 copy.67
  172.1 69.0 %psum.43 = f32[16,768]{1,0:T(8,128)S(1)} all-reduce(f32[16,768]{1,0:T(8,128)S(1)} %fusion.42), channel_id=1, replica_groups=mesh['pb'=16,'sa'=16] {'pb'}, use_global_device_ids=true, to_apply=%region_6.0 | all-reduce | flops 12288 | bytes 98304 | tf_op jit(solution)/shard_map/psum | solution.py:99
  241.1 5.3 fusion.1
  246.5 32.6 %all_gather.24 = f32[256,768]{1,0:T(8,128)} all-gather(f32[16,768]{1,0:T(8,128)S(1)} %bitcast_add_fusion), channel_id=1, replica_groups=mesh['pb'=16,'sa'=16] {'sa'}, dimensions={0}, use_global_device_ids=true | all-gather | bytes 835584 | tf_op jit(solution)/shard_map/all_gather | solution.py:101
  279.1 4.6 multiply_convert_fusion.1
  283.7 2.5 multiply_multiply_fusion.3
  286.3 2.7 fusion.20
  288.9 0.6 copy.68
  289.8 53.6 %psum.42 = f32[16,768]{1,0:T(8,128)S(1)} all-reduce(f32[16,768]{1,0:T(8,128)S(1)} %fusion.41), channel_id=1, replica_groups=mesh['pb'=16,'sa'=16] {'sa'}, use_global_device_ids=true, to_apply=%region_3.0 | all-reduce | flops 12288 | bytes 98304 | tf_op jit(solution)/shard_map/psum | solution.py:98
  343.4 5.4 fusion.3
  348.8 39.3 %all_gather.22 = f32[256,768]{1,0:T(8,128)S(1)} all-gather(f32[16,768]{1,0:T(8,128)S(1)} %bitcast_add_fusion.1), channel_id=1, replica_groups=mesh['pb'=16,'sa'=16] {'pb'}, dimensions={0}, use_global_device_ids=true | all-gather | bytes 835584 | tf_op jit(solution)/shard_map/all_gather | solution.py:100
  388.1 0.9 fusion.43
  389.9 0.9 convolution_multiply_fusion.1
  390.8 1.9 convolution_multiply_fusion
  393.6 2.7 copy.41
  396.3 1.4 fusion.10
  397.8 1.2 copy-done.9
  399.0 2.2 fusion.46
  402.4 4.4 copy.44
  408.2 3.7 fusion.16
  412.2 4.9 multiply_reduce_fusion.1
  417.2 2.8 multiply_reduce_fusion
  420.0 81.8 %all-reduce.1 = (f32[768]{0:T(1024)}, f32[768]{0:T(1024)}) all-reduce(f32[768]{0:T(1024)S(1)} %multiply_reduce_fusion.1, f32[768]{0:T(1024)S(1)} %multiply_reduce_fusion), channel_id=1, replica_groups=mesh['pb'=16,'sa'=16] {'pb','sa'}, use_global_device_ids=true, to_apply=%region_17.0 | all-reduce | flops 1536 | bytes 12288 | tf_op jit(solution)/shard_map/psum | solution.py:136
  501.8 16.7 %all_gather.27 = f32[256,192]{1,0:T(8,128)S(1)} all-gather(f32[16,192]{1,0:T(8,128)S(1)} %bitcast.132), channel_id=1, replica_groups=mesh['pb'=16,'sa'=16] {'sa'}, dimensions={0}, use_global_device_ids=true | all-gather | bytes 208896 | tf_op jit(solution)/shard_map/all_gather | solution.py:103
  518.5 5.5 fusion.47
  524.1 37.7 %all_gather.26 = f32[256,192]{1,0:T(8,128)S(1)} all-gather(f32[16,192]{1,0:T(8,128)S(1)} %bitcast.133), channel_id=1, replica_groups=mesh['pb'=16,'sa'=16] {'pb'}, dimensions={0}, use_global_device_ids=true | all-gather | bytes 208896 | tf_op jit(solution)/shard_map/all_gather | solution.py:102
  561.8 1.5 fusion.45
  563.4 1.5 fusion.44
  564.9 128.9 %all-reduce.7.cloned.1.call-done = f32[768,192]{0,1:T(8,128)} async-done(((f32[768,192]{0,1:T(8,128)}), f32[768,192]{0,1:T(8,128)}) %all-reduce.7.cloned.1.call-update) | async-done | bytes 589840 | tf_op jit(solution)/shard_map/psum | solution.py:135
  693.8 1.9 copy.72
  695.7 1.9 copy.73
  (106 shorter events, 5.7 us)
Async XLA Ops:
  7.2 276.5 %copy-start = (bf16[768,192]{0,1:T(8,128)(2,1)S(1)}, bf16[768,192]{0,1:T(8,128)(2,1)}, u32[]{:S(2)}) copy-start(bf16[768,192]{0,1:T(8,128)(2,1)} %param.13) | copy-start | bytes 884740
  7.2 96.4 %all-gather.5.cloned.1.call-start = ((), (), s32[]{:S(2)}) async-start(), calls=%async_computation.1 | async-start | bytes 6684672 | tf_op jit(solution)/shard_map/all_gather | solution.py:87
  7.9 148.0 %all-gather.3.cloned.1.call-start = ((), (), s32[]{:S(2)}) async-start(), calls=%async_computation | async-start | bytes 6684672 | tf_op jit(solution)/shard_map/all_gather | solution.py:86
  8.7 556.3 %all-reduce.5.cloned.1.call-start = ((), (), s32[]{:S(2)}) async-start(), calls=%async_computation.2 | async-start | bytes 1179648 | tf_op jit(solution)/shard_map/psum | solution.py:134
  107.7 54.8 %copy-start.19 = (f32[2,2,8,128]{3,1,2,0:T(2,128)}, f32[2,2,8,128]{3,1,2,0:T(2,128)S(1)}, u32[]{:S(2)}) copy-start(f32[2,2,8,128]{3,1,2,0:T(2,128)S(1)} %copy.38) | copy-start | bytes 49156
  155.9 4.6 copy-start.1
  159.8 119.3 %copy-start.21 = (f32[2,2,8,128]{3,1,2,0:T(2,128)}, f32[2,2,8,128]{3,1,2,0:T(2,128)S(1)}, u32[]{:S(2)}) copy-start(f32[2,2,8,128]{3,1,2,0:T(2,128)S(1)} %copy.36) | copy-start | bytes 49156
  160.5 2.8 copy-start.2
  160.5 2.8 copy-start.28
  162.5 116.6 %copy-start.23 = (f32[2,2,8,128]{3,1,2,0:T(2,128)}, f32[2,2,8,128]{3,1,2,0:T(2,128)S(1)}, u32[]{:S(2)}) copy-start(f32[2,2,8,128]{3,1,2,0:T(2,128)S(1)} %copy.37) | copy-start | bytes 49156
  163.3 1.5 copy-start.15
  164.8 3.8 copy-start.3
  168.6 3.3 copy-start.13
  241.1 38.0 %copy-start.29 = (f32[768]{0:T(1024)S(1)}, f32[768]{0:T(1024)}, u32[]{:S(2)}) copy-start(f32[768]{0:T(1024)} %param.15) | copy-start | bytes 9220
  283.7 2.6 copy-start.4
  286.3 3.3 copy-start.11
  343.3 44.7 %copy-start.5 = (f32[256,768]{1,0:T(8,128)S(1)}, f32[256,768]{1,0:T(8,128)}, u32[]{:S(2)}) copy-start(f32[256,768]{1,0:T(8,128)} %all_gather.24) | copy-start | bytes 2359300
  343.4 45.7 %copy-start.27 = (s32[256]{0:T(256)S(1)}, s32[256]{0:T(256)}, u32[]{:S(2)}) copy-start(s32[256]{0:T(256)} %all-reduce) | copy-start | bytes 3076
  348.8 43.9 %copy-start.12 = (bf16[192,768]{1,0:T(8,128)(2,1)S(1)}, bf16[192,768]{1,0:T(8,128)(2,1)}, u32[]{:S(2)}) copy-start(bf16[192,768]{1,0:T(8,128)(2,1)} %param.14) | copy-start | bytes 884740
  390.8 1.9 copy-start.6
  393.5 2.8 copy-start.18
  393.6 5.4 slice-start.4
  396.3 2.6 slice-start.5
  397.8 1.2 copy-start.9
  399.0 2.6 copy-start.8
  399.0 2.6 copy-start.14
  401.3 292.6 %all-reduce.7.cloned.1.call-start = ((), (), s32[]{:S(2)}) async-start(), calls=%async_computation.3 | async-start | bytes 1179648 | tf_op jit(solution)/shard_map/psum | solution.py:135
  402.4 5.8 copy-start.17
  402.4 9.5 %slice-start = ((s8[6291456]{0:T(1024)(128)(4,1)}), s8[2097152]{0:T(1024)(128)(4,1)S(1)}, s32[]{:S(2)}) async-start(s8[6291456]{0:T(1024)(128)(4,1)} %bitcast.112), calls=%async_computation.4 | async-start | bytes 4194304
  402.4 9.5 %copy-start.22 = (f32[2,2,8,128]{3,1,2,0:T(2,128)S(1)}, f32[2,2,8,128]{3,1,2,0:T(2,128)}, u32[]{:S(2)}) copy-start(f32[2,2,8,128]{3,1,2,0:T(2,128)} %copy-done.21) | copy-start | bytes 49156
  402.4 9.5 %copy-start.24 = (f32[2,2,8,128]{3,1,2,0:T(2,128)S(1)}, f32[2,2,8,128]{3,1,2,0:T(2,128)}, u32[]{:S(2)}) copy-start(f32[2,2,8,128]{3,1,2,0:T(2,128)} %copy-done.23) | copy-start | bytes 49156
  408.2 4.1 slice-start.1
  408.2 9.0 %slice-start.2 = ((s8[6291456]{0:T(1024)(128)(4,1)}), s8[4194304]{0:T(1024)(128)(4,1)S(1)}, s32[]{:S(2)}) async-start(s8[6291456]{0:T(1024)(128)(4,1)} %bitcast.114), calls=%async_computation.6 | async-start | bytes 8388608
  412.2 4.9 copy-start.10
  412.2 5.0 slice-start.3
  412.2 5.0 copy-start.16
  412.2 5.0 copy-start.20
  417.2 84.6 %copy-start.25 = (f32[16,1,192]{2,0,1:T(8,128)S(1)}, f32[16,1,192]{2,0,1:T(8,128)}, u32[]{:S(2)}) copy-start(f32[16,1,192]{2,0,1:T(8,128)} %copy.67) | copy-start | bytes 36868
  518.5 5.6 copy-start.26
  518.5 44.9 %copy-start.7 = (f32[256,768]{1,0:T(8,128)S(1)}, f32[256,768]{1,0:T(8,128)}, u32[]{:S(2)}) copy-start(f32[256,768]{1,0:T(8,128)} %copy-done.6) | copy-start | bytes 2359300
Sparse Core Ops, SparseCore 0:
  10.5 93.0 all-gather.4
  105.5 50.4 all-gather.2
  401.4 159.6 all-reduce.4
  564.3 129.4 all-reduce.6
where the time goes:
time: 713 us; the launch traced here: 706 us
  blocking collectives  350 us (49%)
  waiting for transfers between devices  249 us (35%)
  matrix products  45.8 us (6%)
  other arithmetic  25 us (4%)
  local copies, waits for them, and re-layouts  18.6 us (3%)
  between operations  17.6 us (2%)
    psum x1, waiting for transfers between devices, per_device(): s_inner_grad = lax.psum(s_inner_part, 'sa')  129 us
    psum x1, blocking collectives, per_device(): lax.psum((q_gain_part, s_gain_part), ('pb', 'sa'))  81.8 us
    all_gather x1, waiting for transfers between devices, per_device(): s_tokens = lax.all_gather(sql_states, 'pb', axis=1, tiled=True)[0]  70.1 us
    psum x1, blocking collectives, per_device(): lax.psum(jnp.dot(s_pooled, s_outer_f, precision=HIGH), 'pb') + s_resid  69 us
    psum x1, blocking collectives, per_device(): lax.psum(jnp.dot(q_pooled, q_outer_f, precision=HIGH), 'sa') + q_resid  53.6 us
    all_gather x1, waiting for transfers between devices, per_device(): q_tokens = lax.all_gather(question_states, 'sa', axis=1, tiled=True)[0]  48.2 us
    all_gather x1, blocking collectives, per_device(): q_embed = lax.all_gather(q_block, 'pb', axis=0, tiled=True)  39.3 us
    all_gather x1, blocking collectives, per_device(): q_pooled_all = lax.all_gather(q_pooled, 'pb', axis=0, tiled=True)  37.7 us
  transfers between devices with their start and end apart: 4, of which 3 were waited for; matrix products, arithmetic and copies ran while one was open for 5% of the time, Pallas kernels for 0%

commit v1 on v0

--- a/solution.py
+++ b/solution.py
@@ -98,7 +98,9 @@
     q_block = lax.psum(jnp.dot(q_pooled, q_outer_f, precision=HIGH), "sa") + q_resid
     s_block = lax.psum(jnp.dot(s_pooled, s_outer_f, precision=HIGH), "pb") + s_resid
     q_embed = lax.all_gather(q_block, "pb", axis=0, tiled=True)
-    s_embed = lax.all_gather(s_block, "sa", axis=0, tiled=True)
+    s_embed = jnp.concatenate(
+        lax.all_to_all(jnp.stack([s_block] * lax.axis_size("sa")), "sa", 0, 0), axis=0
+    )
     q_pooled_all = lax.all_gather(q_pooled, "pb", axis=0, tiled=True)
     s_pooled_all = lax.all_gather(s_pooled, "sa", axis=0, tiled=True)
     positive_all = lax.all_gather(positive_column, "pb", axis=0, tiled=True)

time: 713 us -> 770 us (1.080)
  waiting for transfers between devices: 249 us -> 308 us
  blocking collectives: 350 us -> 327 us
  starting transfers between devices: 0.37 us -> 19.4 us
    psum x1, waiting for transfers between devices: 0.01 us -> 55.2 us  [per_device(): q_inner_grad = lax.psum(q_inner_part, 'pb')]
    all_gather x1 -> x0, blocking collectives: 32.6 us -> none  [per_device(): s_embed = lax.all_gather(s_block, 'sa', axis=0, tiled=True)]
    all_to_all x0 -> x1, starting transfers between devices: none -> 19.1 us  [per_device(): lax.all_to_all(jnp.stack([s_block] * lax.axis_size('sa')), 'sa', 0, 0)]
    psum x1, blocking collectives: 81.8 us -> 90.3 us  [per_device(): lax.psum((q_gain_part, s_gain_part), ('pb', 'sa'))]
    unnamed x86 -> x84, local copies, waits for them, and re-layouts: 16.4 us -> 15.6 us
  transfers between devices with their start and end apart: 4 -> 5, of which waited for: 3 -> 4; matrix products, arithmetic and copies ran while one was open for 5% -> 6% of each run, Pallas kernels for 0% -> 0%
where the time goes in v1:
time: 770 us; the launch traced here: 761 us
  blocking collectives  327 us (42%)
  waiting for transfers between devices  308 us (40%)
  matrix products  48.4 us (6%)
  other arithmetic  22.7 us (3%)
  starting transfers between devices  19.4 us (3%)
  local copies, waits for them, and re-layouts  18.8 us (2%)
  between operations  17.6 us (2%)
    psum x1, waiting for transfers between devices, per_device(): s_inner_grad = lax.psum(s_inner_part, 'sa')  133 us
    psum x1, blocking collectives, per_device(): lax.psum((q_gain_part, s_gain_part), ('pb', 'sa'))  90.3 us
    all_gather x1, waiting for transfers between devices, per_device(): s_tokens = lax.all_gather(sql_states, 'pb', axis=1, tiled=True)[0]  70.1 us
    psum x1, blocking collectives, per_device(): lax.psum(jnp.dot(s_pooled, s_outer_f, precision=HIGH), 'pb') + s_resid  69 us
    psum x1, waiting for transfers between devices, per_device(): q_inner_grad = lax.psum(q_inner_part, 'pb')  55.2 us
    psum x1, blocking collectives, per_device(): lax.psum(jnp.dot(q_pooled, q_outer_f, precision=HIGH), 'sa') + q_resid  52.3 us
    all_gather x1, waiting for transfers between devices, per_device(): q_tokens = lax.all_gather(question_states, 'sa', axis=1, tiled=True)[0]  48.2 us
    all_gather x1, blocking collectives, per_device(): q_embed = lax.all_gather(q_block, 'pb', axis=0, tiled=True)  40.2 us
  transfers between devices with their start and end apart: 5, of which 4 were waited for; matrix products, arithmetic and copies ran while one was open for 6% of the time, Pallas kernels for 0%

profile of v1, /device:TPU:25, one launch (start us, length us, event | category | flops | bytes accessed | tf_op | source)
XLA Modules:
  0.0 761.2 jit_solution(293692618471218624)
XLA Ops:
  7.2 0.7 all-gather.5.cloned.1.call-update
  8.0 0.7 all-gather.3.cloned.1.call-update
  8.7 0.7 convert_bitcast_fusion.2
  9.4 0.7 convert_bitcast_fusion
  10.6 1.3 dynamic-slice
  13.7 0.8 dynamic-update-slice
  14.6 18.9 %all-reduce = s32[256]{0:T(256)} all-reduce(s32[256]{0:T(256)S(1)} %dynamic-update-slice), channel_id=1, replica_groups=mesh['pb'=16,'sa'=16] {'pb'}, use_global_device_ids=true, to_apply=%add | all-reduce | flops 256 | bytes 2048
  33.5 70.1 %all-gather.5.cloned.1.call-done = bf16[1,16,256,768]{3,2,0,1:T(8,128)(2,1)} async-done(((bf16[1,1,256,768]{3,2,0,1:T(8,128)(2,1)}), bf16[1,16,256,768]{3,2,0,1:T(8,128)(2,1)}) %all-gather.5.cloned.1.call-update) | async-done | bytes 6291472 | tf_op jit(solution)/shard_map/all_gather | solution.py:87
  103.6 4.1 multiply_reduce_fusion.2
  107.7 48.2 %all-gather.3.cloned.1.call-done = bf16[1,16,256,768]{3,2,0,1:T(8,128)(2,1)} async-done(((bf16[1,1,256,768]{3,2,0,1:T(8,128)(2,1)}), bf16[1,16,256,768]{3,2,0,1:T(8,128)(2,1)}) %all-gather.3.cloned.1.call-update) | async-done | bytes 6291472 | tf_op jit(solution)/shard_map/all_gather | solution.py:86
  155.9 3.8 convert_reduce_fusion
  160.5 1.9 multiply_reduce_fusion.3
  163.3 1.5 multiply_convert_fusion
  164.8 3.5 multiply_multiply_fusion.2
  168.3 2.7 fusion.17
  171.9 69.0 %psum.43 = f32[16,768]{1,0:T(8,128)S(1)} all-reduce(f32[16,768]{1,0:T(8,128)S(1)} %fusion.42), channel_id=1, replica_groups=mesh['pb'=16,'sa'=16] {'pb'}, use_global_device_ids=true, to_apply=%region_6.0 | all-reduce | flops 12288 | bytes 98304 | tf_op jit(solution)/shard_map/psum | solution.py:99
  240.8 5.4 fusion.1
  246.2 1.0 stack.2
  247.2 19.1 %all-to-all-start = ((f32[16,16,768]{2,1,0:T(8,128)}), f32[16,16,768]{2,1,0:T(8,128)}, u32[]{:S(2)}, u32[]{:S(2)}) async-start(f32[16,16,768]{2,1,0:T(8,128)} %stack.2), calls=%async_computation | async-start | bytes 1572864 | tf_op jit(solution)/shard_map/all_to_all | solution.py:102
  266.3 4.6 multiply_convert_fusion.1
  270.9 3.7 multiply_multiply_fusion.3
  274.6 2.7 fusion.20
  278.2 52.3 %psum.42 = f32[16,768]{1,0:T(8,128)S(1)} all-reduce(f32[16,768]{1,0:T(8,128)S(1)} %fusion.41), channel_id=1, replica_groups=mesh['pb'=16,'sa'=16] {'sa'}, use_global_device_ids=true, to_apply=%region_3.0 | all-reduce | flops 12288 | bytes 98304 | tf_op jit(solution)/shard_map/psum | solution.py:98
  330.5 20.7 %all_gather.23 = f32[256,192]{1,0:T(8,128)} all-gather(f32[16,192]{1,0:T(8,128)} %bitcast.135), channel_id=1, replica_groups=mesh['pb'=16,'sa'=16] {'sa'}, dimensions={0}, use_global_device_ids=true | all-gather | bytes 208896 | tf_op jit(solution)/shard_map/all_gather | solution.py:105
  351.2 35.3 %all_gather.22 = f32[256,192]{1,0:T(8,128)} all-gather(f32[16,192]{1,0:T(8,128)} %bitcast.138), channel_id=1, replica_groups=mesh['pb'=16,'sa'=16] {'pb'}, dimensions={0}, use_global_device_ids=true | all-gather | bytes 208896 | tf_op jit(solution)/shard_map/all_gather | solution.py:104
  386.4 5.3 fusion.3
  391.8 40.2 %all_gather.19 = f32[256,768]{1,0:T(8,128)} all-gather(f32[16,768]{1,0:T(8,128)S(1)} %bitcast_add_fusion.1), channel_id=1, replica_groups=mesh['pb'=16,'sa'=16] {'pb'}, dimensions={0}, use_global_device_ids=true | all-gather | bytes 835584 | tf_op jit(solution)/shard_map/all_gather | solution.py:100
  432.0 2.4 fusion.43
  435.3 2.1 convolution_multiply_fusion.1
  437.3 1.9 convolution_multiply_fusion
  440.1 2.8 copy.41
  442.9 1.4 fusion.10
  444.4 1.2 copy-done.9
  445.6 2.2 fusion.46
  448.1 1.4 fusion.26
  450.0 2.7 copy.44
  452.8 1.4 fusion.16
  454.2 1.1 copy-done.10
  455.4 2.2 fusion.47
  457.7 5.2 multiply_reduce_fusion.1
  463.1 2.6 multiply_reduce_fusion
  467.0 90.3 %all-reduce.1 = (f32[768]{0:T(1024)}, f32[768]{0:T(1024)}) all-reduce(f32[768]{0:T(1024)S(1)} %multiply_reduce_fusion.1, f32[768]{0:T(1024)S(1)} %multiply_reduce_fusion), channel_id=1, replica_groups=mesh['pb'=16,'sa'=16] {'pb','sa'}, use_global_device_ids=true, to_apply=%region_17.0 | all-reduce | flops 1536 | bytes 12288 | tf_op jit(solution)/shard_map/psum | solution.py:138
  557.3 2.7 fusion.45
  560.1 1.5 fusion.44
  561.6 55.2 %all-reduce.5.cloned.1.call-done = f32[768,192]{0,1:T(8,128)} async-done(((f32[768,192]{0,1:T(8,128)}), f32[768,192]{0,1:T(8,128)}) %all-reduce.5.cloned.1.call-update) | async-done | bytes 589840 | tf_op jit(solution)/shard_map/psum | solution.py:136
  616.8 132.7 %all-reduce.7.cloned.1.call-done = f32[768,192]{0,1:T(8,128)} async-done(((f32[768,192]{0,1:T(8,128)}), f32[768,192]{0,1:T(8,128)}) %all-reduce.7.cloned.1.call-update) | async-done | bytes 589840 | tf_op jit(solution)/shard_map/psum | solution.py:137
  749.5 1.9 copy.72
  751.4 1.9 copy.73
  (106 shorter events, 7.7 us)
Async XLA Ops:
  7.2 263.7 %copy-start = (bf16[768,192]{0,1:T(8,128)(2,1)S(1)}, bf16[768,192]{0,1:T(8,128)(2,1)}, u32[]{:S(2)}) copy-start(bf16[768,192]{0,1:T(8,128)(2,1)} %param.13) | copy-start | bytes 884740
  7.2 96.4 %all-gather.5.cloned.1.call-start = ((), (), s32[]{:S(2)}) async-start(), calls=%async_computation.2 | async-start | bytes 6684672 | tf_op jit(solution)/shard_map/all_gather | solution.py:87
  7.9 148.0 %all-gather.3.cloned.1.call-start = ((), (), s32[]{:S(2)}) async-start(), calls=%async_computation.1 | async-start | bytes 6684672 | tf_op jit(solution)/shard_map/all_gather | solution.py:86
  10.3 158.0 %copy-start.17 = (f32[16,256,1]{1,0,2:T(8,128)}, f32[16,256,1]{1,0,2:T(8,128)S(1)}, u32[]{:S(2)}) copy-start(f32[16,256,1]{1,0,2:T(8,128)S(1)} %get-tuple-element.26) | copy-start | bytes 49156
  107.7 55.4 %copy-start.20 = (f32[2,2,8,128]{3,1,2,0:T(2,128)}, f32[2,2,8,128]{3,1,2,0:T(2,128)S(1)}, u32[]{:S(2)}) copy-start(f32[2,2,8,128]{3,1,2,0:T(2,128)S(1)} %copy.38) | copy-start | bytes 49156
  155.9 4.6 copy-start.1
  160.5 2.8 copy-start.2
  160.5 2.8 copy-start.27
  164.8 3.5 copy-start.3
  168.3 3.3 copy-start.14
  240.8 25.5 %copy-start.22 = (f32[2,2,8,128]{3,1,2,0:T(2,128)S(1)}, f32[2,2,8,128]{3,1,2,0:T(2,128)}, u32[]{:S(2)}) copy-start(f32[2,2,8,128]{3,1,2,0:T(2,128)} %copy.36) | copy-start | bytes 49156
  240.8 25.5 %copy-start.24 = (f32[2,2,8,128]{3,1,2,0:T(2,128)S(1)}, f32[2,2,8,128]{3,1,2,0:T(2,128)}, u32[]{:S(2)}) copy-start(f32[2,2,8,128]{3,1,2,0:T(2,128)} %copy.37) | copy-start | bytes 49156
  240.8 25.5 %copy-start.28 = (f32[768]{0:T(1024)S(1)}, f32[768]{0:T(1024)}, u32[]{:S(2)}) copy-start(f32[768]{0:T(1024)} %param.15) | copy-start | bytes 9220
  247.2 184.8 %all-to-all-start = ((f32[16,16,768]{2,1,0:T(8,128)}), f32[16,16,768]{2,1,0:T(8,128)}, u32[]{:S(2)}, u32[]{:S(2)}) async-start(f32[16,16,768]{2,1,0:T(8,128)} %stack.2), calls=%async_computation | async-start | bytes 1572864 | tf_op jit(solution)/shard_map/all_to_all | solution.py:102
  266.3 350.6 %all-reduce.5.cloned.1.call-start = ((), (), s32[]{:S(2)}) async-start(), calls=%async_computation.3 | async-start | bytes 1179648 | tf_op jit(solution)/shard_map/psum | solution.py:136
  270.9 3.7 copy-start.4
  274.6 3.3 copy-start.12
  386.4 47.9 %copy-start.26 = (s32[256]{0:T(256)S(1)}, s32[256]{0:T(256)}, u32[]{:S(2)}) copy-start(s32[256]{0:T(256)} %all-reduce) | copy-start | bytes 3076
  432.0 5.3 copy-start.6
  432.0 7.2 copy-start.13
  437.3 1.9 copy-start.7
  440.1 2.8 copy-start.5
  440.1 2.8 copy-start.19
  440.1 5.5 slice-start.4
  442.9 2.7 slice-start.5
  444.4 1.2 copy-start.9
  447.9 301.6 %all-reduce.7.cloned.1.call-start = ((), (), s32[]{:S(2)}) async-start(), calls=%async_computation.4 | async-start | bytes 1179648 | tf_op jit(solution)/shard_map/psum | solution.py:137
  450.0 2.8 copy-start.18
  450.0 5.4 slice-start.2
  452.8 2.6 slice-start.3
  454.2 1.2 copy-start.10
  455.4 2.3 copy-start.23
  455.4 2.3 copy-start.25
  455.4 7.6 slice-start
  457.7 5.3 slice-start.1
  457.7 5.3 copy-start.11
  457.7 5.3 copy-start.16
  457.7 5.3 copy-start.21
  463.0 97.0 %copy-start.8 = (f32[256,768]{1,0:T(8,128)S(1)}, f32[256,768]{1,0:T(8,128)}, u32[]{:S(2)}) copy-start(f32[256,768]{1,0:T(8,128)} %copy-done.7) | copy-start | bytes 2359300
  463.1 97.0 %copy-start.15 = (f32[256,192]{1,0:T(8,128)S(1)}, f32[256,192]{1,0:T(8,128)}, u32[]{:S(2)}) copy-start(f32[256,192]{1,0:T(8,128)} %all_gather.22) | copy-start | bytes 589828
Sparse Core Ops, SparseCore 0:
  10.5 93.0 all-gather.4
  105.5 50.4 all-gather.2
  448.0 168.7 all-reduce.4
  620.1 129.3 all-reduce.6
